TPU v7x, 32 devices: a whole 2x2x4 slice. The times are simulated.
32 devices in a mesh: runs: 2 (over y), tile: 4 (over z), layer: 2 (over x), star: 2 (over core).
Axes of the slice: x: 2, y: 2, z: 4, core: 2. Of those that a mesh axis runs over, the one named last changes fastest.
Arguments:
- screens: float32 [12, 384, 1536], P(('runs', 'layer'), 'tile'), parts along dimension 0, may hold values from -6 to 6
- layer_weight: float32 [12], P(('runs', 'layer')), parts along dimension 0, may hold values from 0.3 to 1
- wind_row: int32 [12], P('runs'), parts along dimension 0, may hold values from -4 to 4, as said below
- wind_col: int32 [12], P('runs'), parts along dimension 0, may hold values from -4 to 4, as said below
- foot_row: int32 [6, 6], replicated, may hold values from -80 to 79, as said below
- foot_col: int32 [6, 6], replicated, may hold values from -80 to 79, as said below
- frac_row: float32 [6, 6], replicated, may hold values from 0 to 1
- frac_col: float32 [6, 6], replicated, may hold values from 0 to 1
- amplitude: float32 [384, 1536], P('tile', 'layer'), may hold values from 0.5 to 2
- valid: int32 [24, 96], P('tile', 'layer'), may hold values 0 or 1
- recon_matrix: bfloat16 [6, 2, 24, 96, 2688], P('star', None, 'tile', 'layer'), may hold values from -0.0390625 to 0.0390625
- prev_recon: float32 [5376], P('runs'), parts along dimension 0, may hold values from -6 to 6
Outputs:
- shifted: float32 [12, 384, 1536], P(('runs', 'layer'), 'tile'), parts along dimension 0
- slopes: float32 [12, 2, 24, 96], P(('runs', 'star'), None, 'tile', 'layer'), parts along dimension 0
- commands: float32 [5376], P('runs'), parts along dimension 0
There are 2 independent parts, one for each index of `runs`. A program takes and returns all parts, laid end to end along the dimension named above; an argument that names none is the same for every part. Nothing has to cross between parts.
Inputs may be any that keep to these rules, and one draw needn't show every extreme that they name: `wind_row`: some layer takes 4 and another takes -4. `wind_col`: some layer takes 4 and another takes -4. `foot_row`: some star and layer take -80 and another takes 80 - 1. `foot_col`: some star and layer take -80 and another takes 80 - 1.
All inputs are finite; a program needn't handle non-finite values. No bound on the sum of `valid` on one device may be relied on, other than what follows from the above.
Results may differ from a plain program's by a relative error of at most 0.0019.
Values sent between devices are 32-bit elements; how exact they have to be, the bound alone decides.
A program may use at most 64 MiB of HBM per device.

v0:
```python
import math
import jax
import jax.numpy as jnp
from jax import lax
from jax.sharding import PartitionSpec as P

PIX = 16
PAD = 32
WIND = 4
FOOT = 80


def with_halo(value, sides, width):
    for axis, dim in sides:
        size, length = (lax.axis_size(axis), value.shape[dim])
        up = [(i, (i + 1) % size) for i in range(size)]
        down = [(j, i) for i, j in up]
        last = lax.slice_in_dim(value, length - width, length, axis=dim)
        first = lax.slice_in_dim(value, 0, width, axis=dim)
        before = lax.ppermute(last, axis, up)
        after = lax.ppermute(first, axis, down)
        value = jnp.concatenate([before, value, after], axis=dim)
    return value


def roll_columns(values, amount):
    extent = values.shape[-1]
    begin = jnp.mod(-amount, extent)
    doubled = jnp.concatenate([values, values], axis=-1)
    return lax.dynamic_slice_in_dim(doubled, begin, extent, values.ndim - 1)


def sh_slopes(share, amplitude, valid):
    star_count, band_rows, band_cols = share.shape
    sub_rows = band_rows // PIX
    sub_cols = band_cols // PIX
    group = math.gcd(sub_cols, max(1, 128 // PIX))
    blocks = sub_cols // group
    freq_index = jnp.arange(PAD, dtype=jnp.int32)[:, None]
    pixel_index = jnp.arange(PIX, dtype=jnp.int32)[None, :]
    phases = 2.0 * math.pi / PAD * jnp.mod(freq_index * pixel_index, PAD).astype(jnp.float32)
    cosine = jnp.cos(phases)
    sine = jnp.sin(phases)
    identity = jnp.eye(group, dtype=jnp.float32)
    diag_cos = jnp.einsum("gh,vq->gqhv", identity, cosine).reshape(group * PIX, group * PAD)
    diag_sin = jnp.einsum("gh,vq->gqhv", identity, sine).reshape(group * PIX, group * PAD)
    table = jnp.concatenate(
        [
            jnp.concatenate([diag_cos, -diag_sin], axis=1),
            jnp.concatenate([diag_sin, diag_cos], axis=1),
        ],
        axis=0,
    )
    field_real = (amplitude * jnp.cos(share)).reshape(
        star_count, sub_rows, PIX, blocks, group * PIX
    )
    field_imag = (amplitude * jnp.sin(share)).reshape(
        star_count, sub_rows, PIX, blocks, group * PIX
    )
    stacked = jnp.concatenate([field_real, field_imag], axis=-1)
    highest = lax.Precision.HIGHEST
    half = jnp.einsum("sapnk,kj->sapnj", stacked, table, precision=highest)
    row_cos = jnp.einsum("sapnj,up->saunj", half, cosine, precision=highest)
    row_sin = jnp.einsum("sapnj,up->saunj", half, sine, precision=highest)
    width = group * PAD
    spec_real = row_cos[..., :width] + row_sin[..., width:]
    spec_imag = row_cos[..., width:] - row_sin[..., :width]
    intensity = (spec_real * spec_real + spec_imag * spec_imag).reshape(
        star_count, sub_rows, PAD, blocks, group, PAD
    )
    centred = (jnp.mod(jnp.arange(PAD, dtype=jnp.int32) + PAD // 2, PAD) - PAD // 2).astype(
        jnp.float32
    )
    summed = jnp.sum(intensity, axis=(2, 5))
    along_rows = jnp.sum(intensity * centred[None, None, :, None, None, None], axis=(2, 5)) / summed
    along_cols = jnp.sum(intensity * centred[None, None, None, None, None, :], axis=(2, 5)) / summed
    along_rows = along_rows.reshape(star_count, sub_rows, sub_cols)
    along_cols = along_cols.reshape(star_count, sub_rows, sub_cols)
    return jnp.stack([along_rows, along_cols], axis=1) * valid.astype(jnp.float32)


def body(
    screens,
    layer_weight,
    wind_row,
    wind_col,
    foot_row,
    foot_col,
    frac_row,
    frac_col,
    amplitude,
    valid,
    recon_matrix,
    prev_recon,
):
    lay_local, band_rows, extent = screens.shape
    star_local = recon_matrix.shape[0]
    layer_start = lax.axis_index("layer") * lay_local
    star_start = lax.axis_index("star") * star_local
    padded = with_halo(screens, (("tile", 1),), WIND)
    moved = []
    for j in range(lay_local):
        rolled = roll_columns(padded[j], wind_col[layer_start + j])
        moved.append(
            lax.dynamic_slice_in_dim(rolled, WIND - wind_row[layer_start + j], band_rows, 0)
        )
    shifted = jnp.stack(moved)
    source = with_halo(shifted, (("tile", 1),), FOOT)
    pupils = []
    for g in range(star_local):
        star_id = star_start + g
        pupil = jnp.zeros((band_rows, extent), jnp.float32)
        for j in range(lay_local):
            layer_id = layer_start + j
            row_frac = frac_row[star_id, layer_id]
            col_frac = frac_col[star_id, layer_id]
            rows_cut = lax.dynamic_slice_in_dim(
                source[j], FOOT + foot_row[star_id, layer_id], band_rows + 1, 0
            )
            doubled = jnp.concatenate([rows_cut, rows_cut], axis=1)
            window = lax.dynamic_slice_in_dim(
                doubled, jnp.mod(foot_col[star_id, layer_id], extent), extent + 1, 1
            )
            anchor = window[:-1, :-1]
            beside = window[:-1, 1:]
            lower = window[1:, :-1]
            corner = window[1:, 1:]
            sampled = (
                (1.0 - row_frac) * (1.0 - col_frac) * anchor
                + row_frac * (1.0 - col_frac) * lower
                + (1.0 - row_frac) * col_frac * beside
                + row_frac * col_frac * corner
            )
            pupil = pupil + layer_weight[j] * sampled
        pupils.append(pupil)
    partial_value = jnp.stack(pupils)
    block_cols = extent // lax.axis_size("layer")
    summed = lax.psum(partial_value, "layer")
    share = lax.dynamic_slice_in_dim(summed, lax.axis_index("layer") * block_cols, block_cols, 2)
    slopes = sh_slopes(share, amplitude, valid)
    local_terms = jnp.dot(
        slopes.astype(jnp.bfloat16).reshape(1, -1),
        recon_matrix.reshape(-1, recon_matrix.shape[-1]),
        preferred_element_type=jnp.float32,
    )[0]
    recon = lax.psum(local_terms, ("tile", "layer", "star"))
    commands = 2.0 * recon - prev_recon
    return (shifted, slopes, commands)


def solution(mesh):
    return jax.shard_map(
        body,
        mesh=mesh,
        in_specs=(
            P(("runs", "layer"), "tile", None),
            P(("runs", "layer")),
            P("runs"),
            P("runs"),
            P(),
            P(),
            P(),
            P(),
            P("tile", "layer"),
            P("tile", "layer"),
            P("star", None, "tile", "layer", None),
            P("runs"),
        ),
        out_specs=(
            P(("runs", "layer"), "tile", None),
            P(("runs", "star"), None, "tile", "layer"),
            P("runs"),
        ),
        check_vma=False,
    )
```

profile of v0, /device:TPU:0, one launch (start us, length us, event | category | flops | bytes accessed | tf_op | source)
XLA Modules:
  0.0 263.3 jit_solution(9699940544491723572)
XLA Ops:
  7.2 1.0 fusion.100
  8.2 3.1 %collective-permute-start = (f32[3,4,1536]{2,1,0:T(4,128)S(1)}, f32[3,4,1536]{2,1,0:T(4,128)S(1)}, u32[]{:S(2)}, u32[]{:S(2)}) collective-permute-start(f32[3,4,1536]{2,1,0:T(4,128)S(1)} %get-tuple-element.24), channel_id=1, source_target_pairs={{0,4},{4,8},{8,12},{12,0},{1,5},{5,9},{9,13},{13,1},{2,6},{6,10},{... | collective-permute-start | bytes 221192 | tf_op jit(solution)/shard_map/ppermute | solution.py:20
  11.3 2.1 collective-permute-start.1
  13.4 1.5 fusion.107
  20.8 1.7 pad_maximum_fusion.1
  24.0 2.1 fusion.99
  26.1 3.8 %collective-permute-start.3 = (f32[3,80,1536]{2,1,0:T(8,128)}, f32[3,80,1536]{2,1,0:T(8,128)}, u32[]{:S(2)}, u32[]{:S(2)}) collective-permute-start(f32[3,80,1536]{2,1,0:T(8,128)} %get-tuple-element.23), channel_id=1, source_target_pairs={{4,0},{8,4},{12,8},{0,12},{5,1},{9,5},{13,9},{1,13},{6,2},{10,6},{... | collective-permute-start | bytes 4423688 | tf_op jit(solution)/shard_map/ppermute | solution.py:21
  30.0 0.7 fusion.104
  44.1 0.7 fusion.102
  82.5 0.6 fusion.106
  83.2 8.6 %collective-permute-done.3 = f32[3,80,1536]{2,1,0:T(8,128)} collective-permute-done((f32[3,80,1536]{2,1,0:T(8,128)}, f32[3,80,1536]{2,1,0:T(8,128)}, u32[]{:S(2)}, u32[]{:S(2)}) %collective-permute-start.3) | collective-permute-done | bytes 1474592 | tf_op jit(solution)/shard_map/ppermute | solution.py:21
  91.8 1.6 pad_maximum_fusion
  94.0 0.4 fusion.15
  94.6 0.4 fusion.16
  95.2 0.4 fusion.14
  95.6 0.4 fusion.12
  96.0 0.4 fusion.13
  96.4 0.4 fusion.11
  98.1 3.0 %fusion.56 = f32[1,96,1536]{2,1,0:T(8,128)S(1)} fusion(f32[97,1537]{1,0:T(8,128)S(1)} %fusion.14, f32[97,1537]{1,0:T(8,128)S(1)} %fusion.15, f32[97,1537]{1,0:T(8,128)S(1)} %fusion.16, f32[]{:T(128)S(6)} %mul.523, f32[]{:T(128)S(6)} %mul.520, f32[]{:T(128)S(6)} %mul.517, f32[]{:T(128)S(6)} %mul.514, f32[]{:T(128)} %bitcast.31, f32[]{:T(128)S(6)} %mul.509, ...), kind=kLoop, calls=%fused_computation.130 | loop fusion | flops 3833856 | bytes 7667772 | tf_op jit(solution)/shard_map/stack | solution.py:136
  101.1 3.0 %fusion.41 = f32[1,96,1536]{2,1,0:T(8,128)S(1)} fusion(f32[97,1537]{1,0:T(8,128)S(1)} %fusion.11, f32[97,1537]{1,0:T(8,128)S(1)} %fusion.12, f32[97,1537]{1,0:T(8,128)S(1)} %fusion.13, f32[]{:T(128)S(6)} %mul.562, f32[]{:T(128)S(6)} %mul.559, f32[]{:T(128)S(6)} %mul.556, f32[]{:T(128)S(6)} %mul.553, f32[]{:T(128)S(6)} %mul.549, f32[]{:T(128)S(6)} %mul.546, ...), kind=kLoop, calls=%fused_computation.103 | loop fusion | flops 3833856 | bytes 7667772 | tf_op jit(solution)/shard_map/stack | solution.py:136
  104.1 3.0 %fusion.26 = f32[1,96,1536]{2,1,0:T(8,128)S(1)} fusion(f32[97,1537]{1,0:T(8,128)S(1)} %fusion.8, f32[97,1537]{1,0:T(8,128)S(1)} %fusion.9, f32[97,1537]{1,0:T(8,128)S(1)} %fusion.10, f32[]{:T(128)S(6)} %mul.601, f32[]{:T(128)S(6)} %mul.598, f32[]{:T(128)S(6)} %mul.595, f32[]{:T(128)S(6)} %mul.592, f32[]{:T(128)S(6)} %mul.588, f32[]{:T(128)S(6)} %mul.585, ...), kind=kLoop, calls=%fused_computation.76 | loop fusion | flops 3833856 | bytes 7667772 | tf_op jit(solution)/shard_map/stack | solution.py:136
  107.1 1.3 pad_maximum_fusion.3
  109.2 55.3 %all-reduce.2.cloned.1.call-done = f32[3,96,1536]{2,1,0:T(8,128)} async-done(((f32[3,96,1536]{2,1,0:T(8,128)}), f32[3,96,1536]{2,1,0:T(8,128)}) %all-reduce.2.cloned.1.call-update) | async-done | bytes 1769488 | tf_op jit(solution)/shard_map/psum | solution.py:138
  164.5 5.2 %cosine_multiply_fusion = (f32[3,96,768]{2,1,0:T(8,128)S(1)}, f32[3,96,768]{2,1,0:T(8,128)S(1)}) fusion(f32[3,96,1536]{2,1,0:T(8,128)} %all-reduce.2.cloned.1.call-done, s32[]{:T(128)S(6)} %select_n.305, f32[96,768]{1,0:T(8,128)} %param.20), kind=kLoop, calls=%fused_computation.44 | loop fusion | flops 442368 | bytes 2949124 | tf_op jit(solution)/shard_map/mul | solution.py:54
  170.3 3.1 %fusion.3 = f32[3,6,16,6,512]{4,2,3,1,0:T(8,128)S(1)} fusion(f32[3,6,16,6,128]{4,2,3,1,0:T(8,128)S(1)} %copy.19, f32[3,6,16,6,128]{4,2,3,1,0:T(8,128)S(1)} %copy.18, f32[128,256]{1,0:T(8,128)S(1)} %reshape.193, f32[128,256]{1,0:T(8,128)S(1)} %reshape.194, f32[128,256]{1,0:T(8,128)S(1)} %neg.18), kind=kOutput, calls=%fused_computation.14 | convolution fusion | flops 2718744576 | bytes 5701632 | tf_op jit(solution)/shard_map/sapnk,kj->sapnj/dot_general | solution.py:62
  173.4 5.8 %convolution_bitcast_fusion.1 = f32[3,6,32,6,512]{4,2,3,1,0:T(8,128)S(1)} fusion(f32[3,6,16,6,512]{4,2,3,1,0:T(8,128)S(1)} %fusion.3), kind=kOutput, calls=%fused_computation.9 | convolution fusion | flops 339745792 | bytes 10616832 | tf_op jit(solution)/shard_map/sapnj,up->saunj/dot_general | solution.py:64
  179.1 6.0 %convolution_bitcast_fusion.2 = f32[3,6,32,6,512]{4,2,3,1,0:T(8,128)S(1)} fusion(f32[3,6,16,6,512]{4,2,3,1,0:T(8,128)S(1)} %fusion.3), kind=kOutput, calls=%fused_computation.10 | convolution fusion | flops 339745792 | bytes 10616832 | tf_op jit(solution)/shard_map/sapnj,up->saunj/dot_general | solution.py:63
  185.2 3.4 %multiply_reduce_fusion.1 = (f32[3,6,6,256]{3,2,1,0:T(8,128)S(1)}, f32[3,6,6,256]{3,2,1,0:T(8,128)S(1)}, f32[3,6,6,256]{3,2,1,0:T(8,128)S(1)}) fusion(f32[32]{0:T(128)S(1)} %fusion.89, f32[256]{0:T(256)S(1)} %mul.613, f32[3,6,32,6,512]{4,2,3,1,0:T(8,128)S(1)} %convolution_bitcast_fusion.1, f32[3,6,32,6,512]{4,2,3,1,0:T(8,128)S(1)} %convolution_bitcast_fusion.2), kind=kLoop, calls=%fused_computation.7 | loop fusion | flops 8764416 | bytes 14488704 | tf_op jit(solution)/shard_map/reduce_sum | solution.py:75
  189.8 5.3 %fusion.7 = f32[2688]{0:T(1024)S(1)} fusion(bf16[3,2,6,48,2688]{4,3,2,1,0:T(8,128)(2,1)} %param.22, bf16[3,2,6,48,1]{3,2,0,1,4:T(8,128)(2,1)S(1)} %get-tuple-element.12), kind=kOutput, calls=%fused_computation.42 | convolution fusion | flops 9289728 | bytes 9303936 | tf_op jit(solution)/shard_map/dot_general | solution.py:141
  195.1 60.1 %psum.15 = f32[2688]{0:T(1024)S(1)} all-reduce(f32[2688]{0:T(1024)S(1)} %fusion.7), channel_id=1, replica_groups=mesh['runs'=2,'tile'=4,'layer'=2,'star'=2] {'tile','layer','star'}, use_global_device_ids=true, to_apply=%region_7.8 | all-reduce | flops 2688 | bytes 21504 | tf_op jit(solution)/shard_map/psum | solution.py:146
  255.2 0.6 copy.20
  255.8 0.6 multiply_subtract_fusion
  (58 shorter events, 6.1 us)
Async XLA Ops:
  7.2 157.3 %all-reduce.2.cloned.1.call-start = ((), (), s32[]{:S(2)}) async-start(), calls=%async_computation | async-start | bytes 3538944 | tf_op jit(solution)/shard_map/psum | solution.py:138
  8.2 12.5 %collective-permute-start = (f32[3,4,1536]{2,1,0:T(4,128)S(1)}, f32[3,4,1536]{2,1,0:T(4,128)S(1)}, u32[]{:S(2)}, u32[]{:S(2)}) collective-permute-start(f32[3,4,1536]{2,1,0:T(4,128)S(1)} %get-tuple-element.24), channel_id=1, source_target_pairs={{0,4},{4,8},{8,12},{12,0},{1,5},{5,9},{9,13},{13,1},{2,6},{6,10},{... | collective-permute-start | bytes 221192 | tf_op jit(solution)/shard_map/ppermute | solution.py:20
  11.3 9.4 %collective-permute-start.1 = (f32[3,4,1536]{2,1,0:T(4,128)S(1)}, f32[3,4,1536]{2,1,0:T(4,128)S(1)}, u32[]{:S(2)}, u32[]{:S(2)}) collective-permute-start(f32[3,4,1536]{2,1,0:T(4,128)S(1)} %get-tuple-element.25), channel_id=1, source_target_pairs={{4,0},{8,4},{12,8},{0,12},{5,1},{9,5},{13,9},{1,13},{6,2},{10,6},{... | collective-permute-start | bytes 221192 | tf_op jit(solution)/shard_map/ppermute | solution.py:21
  23.9 2.2 copy-start
  23.9 6.0 %copy-start.2 = (s32[6,6]{1,0:T(8,128)S(1)}, s32[6,6]{1,0:T(8,128)}, u32[]{:S(2)}) copy-start(s32[6,6]{1,0:T(8,128)} %param.16) | copy-start | bytes 436
  24.0 6.0 %copy-start.3 = (s32[6,6]{1,0:T(8,128)S(1)}, s32[6,6]{1,0:T(8,128)}, u32[]{:S(2)}) copy-start(s32[6,6]{1,0:T(8,128)} %param.17) | copy-start | bytes 436
  24.0 20.1 %copy-start.4 = (f32[6,6]{1,0:T(8,128)S(1)}, f32[6,6]{1,0:T(8,128)}, u32[]{:S(2)}) copy-start(f32[6,6]{1,0:T(8,128)} %param.19) | copy-start | bytes 436
  24.0 20.1 %copy-start.5 = (f32[6,6]{1,0:T(8,128)S(1)}, f32[6,6]{1,0:T(8,128)}, u32[]{:S(2)}) copy-start(f32[6,6]{1,0:T(8,128)} %param.18) | copy-start | bytes 436
  24.0 58.5 %copy-start.6 = (f32[3]{0:T(128)S(1)}, f32[3]{0:T(128)}, u32[]{:S(2)}) copy-start(f32[3]{0:T(128)} %param.13) | copy-start | bytes 40
  26.1 57.0 %collective-permute-start.2 = (f32[3,80,1536]{2,1,0:T(8,128)}, f32[3,80,1536]{2,1,0:T(8,128)S(1)}, u32[]{:S(2)}, u32[]{:S(2)}) collective-permute-start(f32[3,80,1536]{2,1,0:T(8,128)} %get-tuple-element.22), channel_id=1, source_target_pairs={{0,4},{4,8},{8,12},{12,0},{1,5},{5,9},{9,13},{13,1},{2,6},{6,10},{... | collective-permute-start | bytes 4423688 | tf_op jit(solution)/shard_map/ppermute | solution.py:20
  26.1 65.7 %collective-permute-start.3 = (f32[3,80,1536]{2,1,0:T(8,128)}, f32[3,80,1536]{2,1,0:T(8,128)}, u32[]{:S(2)}, u32[]{:S(2)}) collective-permute-start(f32[3,80,1536]{2,1,0:T(8,128)} %get-tuple-element.23), channel_id=1, source_target_pairs={{4,0},{8,4},{12,8},{0,12},{5,1},{9,5},{13,9},{1,13},{6,2},{10,6},{... | collective-permute-start | bytes 4423688 | tf_op jit(solution)/shard_map/ppermute | solution.py:21
  108.4 0.7 copy-start.7
  189.8 66.0 %copy-start.1 = (f32[2688]{0:T(1024)S(1)}, f32[2688]{0:T(1024)}, u32[]{:S(2)}) copy-start(f32[2688]{0:T(1024)} %param.23) | copy-start | bytes 32260
Sparse Core Ops, SparseCore 0:
  108.5 55.8 all-reduce.1
where the time goes:
time: 265 us; the launch traced here: 263 us
  between operations  71.4 us (27%)
  waiting for transfers between devices  63.9 us (24%)
  blocking collectives  60.1 us (23%)
  other arithmetic  28.6 us (11%)
  matrix products  20.2 us (8%)
  local copies, waits for them, and re-layouts  9.96 us (4%)
  starting transfers between devices  9.06 us (3%)
    psum x1, blocking collectives, body(): recon = lax.psum(local_terms, ('tile', 'layer', 'star'))  60.1 us
    psum x1, waiting for transfers between devices, body(): summed = lax.psum(partial_value, 'layer')  55.3 us
    another operation x4, other arithmetic, body(): partial_value = jnp.stack(pupils)  10.2 us
    ppermute x2, waiting for transfers between devices, with_halo(): after = lax.ppermute(first, axis, down)  8.64 us
    dot_general x1, matrix products, sh_slopes(): row_cos = jnp.einsum('sapnj,up->saunj', half, cosine, precision=highest)  6.05 us
    ppermute x2, starting transfers between devices, with_halo(): after = lax.ppermute(first, axis, down)  5.91 us
    dot_general x1, matrix products, sh_slopes(): row_sin = jnp.einsum('sapnj,up->saunj', half, sine, precision=highest)  5.76 us
  transfers between devices with their start and end apart: 5, of which 2 were waited for; matrix products, arithmetic and copies ran while one was open for 2% of the time, Pallas kernels for 0%

commit v1 on v0

--- a/solution.py
+++ b/solution.py
@@ -143,7 +143,8 @@
         recon_matrix.reshape(-1, recon_matrix.shape[-1]),
         preferred_element_type=jnp.float32,
     )[0]
-    recon = lax.psum(local_terms, ("tile", "layer", "star"))
+    partial = lax.psum(local_terms, "tile")
+    recon = lax.psum(partial, ("layer", "star"))
     commands = 2.0 * recon - prev_recon
     return (shifted, slopes, commands)
 

time: 265 us -> 233 us (0.88)
  blocking collectives: 60.1 us -> 28.9 us
    psum x1 -> x2, blocking collectives: 60.1 us -> 28.9 us  [the longest x1 18.7 us: body(): partial = lax.psum(local_terms, 'tile')]
where the time goes in v1:
time: 233 us; the launch traced here: 232 us
  between operations  71.2 us (31%)
  waiting for transfers between devices  63.9 us (27%)
  blocking collectives  28.9 us (12%)
  other arithmetic  28.8 us (12%)
  matrix products  20.2 us (9%)
  local copies, waits for them, and re-layouts  10 us (4%)
  starting transfers between devices  9.06 us (4%)
    psum x1, waiting for transfers between devices, body(): summed = lax.psum(partial_value, 'layer')  55.3 us
    psum x1, blocking collectives, body(): partial = lax.psum(local_terms, 'tile')  18.7 us
    another operation x4, other arithmetic, body(): partial_value = jnp.stack(pupils)  10.4 us
    psum x1, blocking collectives, body(): recon = lax.psum(partial, ('layer', 'star'))  10.2 us
    ppermute x2, waiting for transfers between devices, with_halo(): after = lax.ppermute(first, axis, down)  8.55 us
    dot_general x1, matrix products, sh_slopes(): row_cos = jnp.einsum('sapnj,up->saunj', half, cosine, precision=highest)  6.05 us
    ppermute x2, starting transfers between devices, with_halo(): after = lax.ppermute(first, axis, down)  5.91 us
    dot_general x1, matrix products, sh_slopes(): row_sin = jnp.einsum('sapnj,up->saunj', half, sine, precision=highest)  5.76 us
  transfers between devices with their start and end apart: 5, of which 2 were waited for; matrix products, arithmetic and copies ran while one was open for 2% of the time, Pallas kernels for 0%

profile of v1, /device:TPU:0, one launch (start us, length us, event | category | flops | bytes accessed | tf_op | source)
XLA Modules:
  0.0 232.0 jit_solution(7134538177423129979)
XLA Ops:
  7.2 1.0 fusion.100
  8.2 3.1 %collective-permute-start = (f32[3,4,1536]{2,1,0:T(4,128)S(1)}, f32[3,4,1536]{2,1,0:T(4,128)S(1)}, u32[]{:S(2)}, u32[]{:S(2)}) collective-permute-start(f32[3,4,1536]{2,1,0:T(4,128)S(1)} %get-tuple-element.24), channel_id=1, source_target_pairs={{0,4},{4,8},{8,12},{12,0},{1,5},{5,9},{9,13},{13,1},{2,6},{6,10},{... | collective-permute-start | bytes 221192 | tf_op jit(solution)/shard_map/ppermute | solution.py:20
  11.3 2.1 collective-permute-start.1
  13.4 1.4 fusion.107
  20.5 1.7 pad_maximum_fusion.1
  23.7 2.1 fusion.99
  25.9 3.8 %collective-permute-start.3 = (f32[3,80,1536]{2,1,0:T(8,128)}, f32[3,80,1536]{2,1,0:T(8,128)}, u32[]{:S(2)}, u32[]{:S(2)}) collective-permute-start(f32[3,80,1536]{2,1,0:T(8,128)} %get-tuple-element.23), channel_id=1, source_target_pairs={{4,0},{8,4},{12,8},{0,12},{5,1},{9,5},{13,9},{1,13},{6,2},{10,6},{... | collective-permute-start | bytes 4423688 | tf_op jit(solution)/shard_map/ppermute | solution.py:21
  29.7 0.7 fusion.104
  43.8 0.8 fusion.102
  82.3 0.7 fusion.106
  83.0 8.5 %collective-permute-done.3 = f32[3,80,1536]{2,1,0:T(8,128)} collective-permute-done((f32[3,80,1536]{2,1,0:T(8,128)}, f32[3,80,1536]{2,1,0:T(8,128)}, u32[]{:S(2)}, u32[]{:S(2)}) %collective-permute-start.3) | collective-permute-done | bytes 1474592 | tf_op jit(solution)/shard_map/ppermute | solution.py:21
  91.5 1.6 pad_maximum_fusion
  93.7 0.4 fusion.15
  94.3 0.4 fusion.16
  94.9 0.4 fusion.14
  95.3 0.4 fusion.12
  95.8 0.4 fusion.13
  97.9 3.0 %fusion.56 = f32[1,96,1536]{2,1,0:T(8,128)S(1)} fusion(f32[97,1537]{1,0:T(8,128)S(1)} %fusion.14, f32[97,1537]{1,0:T(8,128)S(1)} %fusion.15, f32[97,1537]{1,0:T(8,128)S(1)} %fusion.16, f32[]{:T(128)S(6)} %mul.523, f32[]{:T(128)S(6)} %mul.520, f32[]{:T(128)S(6)} %mul.517, f32[]{:T(128)S(6)} %mul.514, f32[]{:T(128)} %bitcast.31, f32[]{:T(128)S(6)} %mul.509, ...), kind=kLoop, calls=%fused_computation.130 | loop fusion | flops 3833856 | bytes 7667772 | tf_op jit(solution)/shard_map/stack | solution.py:136
  100.9 3.0 %fusion.41 = f32[1,96,1536]{2,1,0:T(8,128)S(1)} fusion(f32[97,1537]{1,0:T(8,128)S(1)} %fusion.11, f32[97,1537]{1,0:T(8,128)S(1)} %fusion.12, f32[97,1537]{1,0:T(8,128)S(1)} %fusion.13, f32[]{:T(128)S(6)} %mul.562, f32[]{:T(128)S(6)} %mul.559, f32[]{:T(128)S(6)} %mul.556, f32[]{:T(128)S(6)} %mul.553, f32[]{:T(128)S(6)} %mul.549, f32[]{:T(128)S(6)} %mul.546, ...), kind=kLoop, calls=%fused_computation.103 | loop fusion | flops 3833856 | bytes 7667772 | tf_op jit(solution)/shard_map/stack | solution.py:136
  104.0 3.0 %fusion.26 = f32[1,96,1536]{2,1,0:T(8,128)S(1)} fusion(f32[97,1537]{1,0:T(8,128)S(1)} %fusion.8, f32[97,1537]{1,0:T(8,128)S(1)} %fusion.9, f32[97,1537]{1,0:T(8,128)S(1)} %fusion.10, f32[]{:T(128)S(6)} %mul.601, f32[]{:T(128)S(6)} %mul.598, f32[]{:T(128)S(6)} %mul.595, f32[]{:T(128)S(6)} %mul.592, f32[]{:T(128)S(6)} %mul.588, f32[]{:T(128)S(6)} %mul.585, ...), kind=kLoop, calls=%fused_computation.76 | loop fusion | flops 3833856 | bytes 7667772 | tf_op jit(solution)/shard_map/stack | solution.py:136
  107.0 1.3 pad_maximum_fusion.3
  109.1 55.3 %all-reduce.2.cloned.1.call-done = f32[3,96,1536]{2,1,0:T(8,128)} async-done(((f32[3,96,1536]{2,1,0:T(8,128)}), f32[3,96,1536]{2,1,0:T(8,128)}) %all-reduce.2.cloned.1.call-update) | async-done | bytes 1769488 | tf_op jit(solution)/shard_map/psum | solution.py:138
  164.4 5.2 %cosine_multiply_fusion = (f32[3,96,768]{2,1,0:T(8,128)S(1)}, f32[3,96,768]{2,1,0:T(8,128)S(1)}) fusion(f32[3,96,1536]{2,1,0:T(8,128)} %all-reduce.2.cloned.1.call-done, s32[]{:T(128)S(6)} %select_n.305, f32[96,768]{1,0:T(8,128)} %param.20), kind=kLoop, calls=%fused_computation.44 | loop fusion | flops 442368 | bytes 2949124 | tf_op jit(solution)/shard_map/mul | solution.py:54
  170.2 3.1 %fusion.3 = f32[3,6,16,6,512]{4,2,3,1,0:T(8,128)S(1)} fusion(f32[3,6,16,6,128]{4,2,3,1,0:T(8,128)S(1)} %copy.19, f32[3,6,16,6,128]{4,2,3,1,0:T(8,128)S(1)} %copy.18, f32[128,256]{1,0:T(8,128)S(1)} %reshape.193, f32[128,256]{1,0:T(8,128)S(1)} %reshape.194, f32[128,256]{1,0:T(8,128)S(1)} %neg.18), kind=kOutput, calls=%fused_computation.14 | convolution fusion | flops 2718744576 | bytes 5701632 | tf_op jit(solution)/shard_map/sapnk,kj->sapnj/dot_general | solution.py:62
  173.3 5.8 %convolution_bitcast_fusion.1 = f32[3,6,32,6,512]{4,2,3,1,0:T(8,128)S(1)} fusion(f32[3,6,16,6,512]{4,2,3,1,0:T(8,128)S(1)} %fusion.3), kind=kOutput, calls=%fused_computation.9 | convolution fusion | flops 339745792 | bytes 10616832 | tf_op jit(solution)/shard_map/sapnj,up->saunj/dot_general | solution.py:64
  179.0 6.0 %convolution_bitcast_fusion.2 = f32[3,6,32,6,512]{4,2,3,1,0:T(8,128)S(1)} fusion(f32[3,6,16,6,512]{4,2,3,1,0:T(8,128)S(1)} %fusion.3), kind=kOutput, calls=%fused_computation.10 | convolution fusion | flops 339745792 | bytes 10616832 | tf_op jit(solution)/shard_map/sapnj,up->saunj/dot_general | solution.py:63
  185.1 3.4 %multiply_reduce_fusion.1 = (f32[3,6,6,256]{3,2,1,0:T(8,128)S(1)}, f32[3,6,6,256]{3,2,1,0:T(8,128)S(1)}, f32[3,6,6,256]{3,2,1,0:T(8,128)S(1)}) fusion(f32[32]{0:T(128)S(1)} %fusion.89, f32[256]{0:T(256)S(1)} %mul.613, f32[3,6,32,6,512]{4,2,3,1,0:T(8,128)S(1)} %convolution_bitcast_fusion.1, f32[3,6,32,6,512]{4,2,3,1,0:T(8,128)S(1)} %convolution_bitcast_fusion.2), kind=kLoop, calls=%fused_computation.7 | loop fusion | flops 8764416 | bytes 14488704 | tf_op jit(solution)/shard_map/reduce_sum | solution.py:75
  189.7 5.3 %fusion.7 = f32[2688]{0:T(1024)S(1)} fusion(bf16[3,2,6,48,2688]{4,3,2,1,0:T(8,128)(2,1)} %param.22, bf16[3,2,6,48,1]{3,2,0,1,4:T(8,128)(2,1)S(1)} %get-tuple-element.12), kind=kOutput, calls=%fused_computation.42 | convolution fusion | flops 9289728 | bytes 9303936 | tf_op jit(solution)/shard_map/dot_general | solution.py:141
  195.0 18.7 %psum.22 = f32[2688]{0:T(1024)S(1)} all-reduce(f32[2688]{0:T(1024)S(1)} %fusion.7), channel_id=1, replica_groups=mesh['runs'=2,'tile'=4,'layer'=2,'star'=2] {'tile'}, use_global_device_ids=true, to_apply=%region_7.8 | all-reduce | flops 2688 | bytes 21504 | tf_op jit(solution)/shard_map/psum | solution.py:146
  213.7 10.2 %psum.23 = f32[2688]{0:T(1024)S(1)} all-reduce(f32[2688]{0:T(1024)S(1)} %psum.22), channel_id=1, replica_groups=mesh['runs'=2,'tile'=4,'layer'=2,'star'=2] {'layer','star'}, use_global_device_ids=true, to_apply=%region_8.9 | all-reduce | flops 2688 | bytes 21504 | tf_op jit(solution)/shard_map/psum | solution.py:147
  223.9 0.6 copy.20
  224.5 0.6 multiply_subtract_fusion
  (59 shorter events, 6.5 us)
Async XLA Ops:
  7.2 157.2 %all-reduce.2.cloned.1.call-start = ((), (), s32[]{:S(2)}) async-start(), calls=%async_computation | async-start | bytes 3538944 | tf_op jit(solution)/shard_map/psum | solution.py:138
  8.2 12.3 %collective-permute-start = (f32[3,4,1536]{2,1,0:T(4,128)S(1)}, f32[3,4,1536]{2,1,0:T(4,128)S(1)}, u32[]{:S(2)}, u32[]{:S(2)}) collective-permute-start(f32[3,4,1536]{2,1,0:T(4,128)S(1)} %get-tuple-element.24), channel_id=1, source_target_pairs={{0,4},{4,8},{8,12},{12,0},{1,5},{5,9},{9,13},{13,1},{2,6},{6,10},{... | collective-permute-start | bytes 221192 | tf_op jit(solution)/shard_map/ppermute | solution.py:20
  11.3 9.2 %collective-permute-start.1 = (f32[3,4,1536]{2,1,0:T(4,128)S(1)}, f32[3,4,1536]{2,1,0:T(4,128)S(1)}, u32[]{:S(2)}, u32[]{:S(2)}) collective-permute-start(f32[3,4,1536]{2,1,0:T(4,128)S(1)} %get-tuple-element.25), channel_id=1, source_target_pairs={{4,0},{8,4},{12,8},{0,12},{5,1},{9,5},{13,9},{1,13},{6,2},{10,6},{... | collective-permute-start | bytes 221192 | tf_op jit(solution)/shard_map/ppermute | solution.py:21
  23.7 2.2 copy-start
  23.7 6.0 %copy-start.2 = (s32[6,6]{1,0:T(8,128)S(1)}, s32[6,6]{1,0:T(8,128)}, u32[]{:S(2)}) copy-start(s32[6,6]{1,0:T(8,128)} %param.16) | copy-start | bytes 436
  23.7 6.0 %copy-start.3 = (s32[6,6]{1,0:T(8,128)S(1)}, s32[6,6]{1,0:T(8,128)}, u32[]{:S(2)}) copy-start(s32[6,6]{1,0:T(8,128)} %param.17) | copy-start | bytes 436
  23.7 20.1 %copy-start.4 = (f32[6,6]{1,0:T(8,128)S(1)}, f32[6,6]{1,0:T(8,128)}, u32[]{:S(2)}) copy-start(f32[6,6]{1,0:T(8,128)} %param.19) | copy-start | bytes 436
  23.7 20.1 %copy-start.5 = (f32[6,6]{1,0:T(8,128)S(1)}, f32[6,6]{1,0:T(8,128)}, u32[]{:S(2)}) copy-start(f32[6,6]{1,0:T(8,128)} %param.18) | copy-start | bytes 436
  23.7 58.6 %copy-start.6 = (f32[3]{0:T(128)S(1)}, f32[3]{0:T(128)}, u32[]{:S(2)}) copy-start(f32[3]{0:T(128)} %param.13) | copy-start | bytes 40
  25.9 57.1 %collective-permute-start.2 = (f32[3,80,1536]{2,1,0:T(8,128)}, f32[3,80,1536]{2,1,0:T(8,128)S(1)}, u32[]{:S(2)}, u32[]{:S(2)}) collective-permute-start(f32[3,80,1536]{2,1,0:T(8,128)} %get-tuple-element.22), channel_id=1, source_target_pairs={{0,4},{4,8},{8,12},{12,0},{1,5},{5,9},{9,13},{13,1},{2,6},{6,10},{... | collective-permute-start | bytes 4423688 | tf_op jit(solution)/shard_map/ppermute | solution.py:20
  25.9 65.7 %collective-permute-start.3 = (f32[3,80,1536]{2,1,0:T(8,128)}, f32[3,80,1536]{2,1,0:T(8,128)}, u32[]{:S(2)}, u32[]{:S(2)}) collective-permute-start(f32[3,80,1536]{2,1,0:T(8,128)} %get-tuple-element.23), channel_id=1, source_target_pairs={{4,0},{8,4},{12,8},{0,12},{5,1},{9,5},{13,9},{1,13},{6,2},{10,6},{... | collective-permute-start | bytes 4423688 | tf_op jit(solution)/shard_map/ppermute | solution.py:21
  108.3 0.7 copy-start.7
  189.7 34.8 %copy-start.1 = (f32[2688]{0:T(1024)S(1)}, f32[2688]{0:T(1024)}, u32[]{:S(2)}) copy-start(f32[2688]{0:T(1024)} %param.23) | copy-start | bytes 32260
Sparse Core Ops, SparseCore 0:
  108.4 55.8 all-reduce.1
